TPU v7x, 256 devices: a whole 4x4x8 slice. The times are simulated.
256 devices in a mesh: frame: 16 (over x_hi, z), head: 16 (over y, x_lo, core).
Axes of the slice: x: 4 (x_hi: 2, x_lo: 2; x = x_hi * 2 + x_lo), y: 4, z: 8, core: 2. Of those that a mesh axis runs over, the one named last changes fastest.
Arguments:
- query_proj: bfloat16 [16, 24576, 128], P('head', 'frame'), may hold values from -6 to 6
- key_proj: bfloat16 [16, 24576, 128], P('head', 'frame'), may hold values from -6 to 6
- value_proj: bfloat16 [16, 24576, 128], P('head', 'frame'), may hold values from -6 to 6
- lengths: int32 [32], replicated, may hold values from 384 to 1536, as said below
- out_weight: bfloat16 [1024, 1024], P('head'), may hold values from -0.1875 to 0.1875
Outputs:
- projected: bfloat16 [49152, 1024], P(('frame', 'head'))
Inputs may be any that keep to these rules, and one draw needn't show every extreme that they name: `lengths`: some frame has all 1536 tokens valid.
All inputs are finite; a program needn't handle non-finite values.
Results may differ from a plain program's by a relative error of at most 0.0057.
Values may be sent and summed in bfloat16 or wider, within the bound.
A program may use at most 64 MiB of HBM per device.

v0:
```python
import math

import jax
import jax.numpy as jnp
from jax import lax
from jax.sharding import PartitionSpec as P

HS = 64
FT = 1536


def shifted(x, axis, by):
    length = lax.axis_size(axis)
    pairs = [(i, i + by) for i in range(length) if 0 <= i + by < length]
    return lax.ppermute(x, axis, pairs)


def frame_count(lengths, frame_id):
    table = jnp.arange(lengths.shape[0], dtype=jnp.int32)
    return jnp.sum(jnp.where(table == frame_id, lengths, 0))


def attend(queries, key_block, value_block, key_valid, local_heads):
    score_scale = 1.0 / math.sqrt(HS)
    block_rows = min(512, FT)
    block_count = FT // block_rows
    query_blocks = jnp.transpose(
        queries.reshape(local_heads, block_count, block_rows, HS), (1, 0, 2, 3)
    )

    def one_block(query_part):
        scores = (
            jnp.einsum("hqd,hkd->hqk", query_part, key_block, preferred_element_type=jnp.float32)
            * score_scale
        )
        scores = jnp.where(key_valid[None, None, :], scores, -jnp.inf)
        top_score = jnp.max(scores, axis=2, keepdims=True)
        expon = jnp.where(key_valid[None, None, :], jnp.exp(scores - top_score), 0.0)
        weights = (expon / jnp.sum(expon, axis=2, keepdims=True)).astype(jnp.bfloat16)
        result = jnp.einsum(
            "hqk,hkd->qhd", weights, value_block, preferred_element_type=jnp.float32
        )
        return result.astype(jnp.bfloat16).reshape(block_rows, local_heads * HS)

    return lax.map(one_block, query_blocks).reshape(FT, local_heads * HS)


def shards(query_proj, key_proj, value_proj, lengths, out_weight):
    local_heads = query_proj.shape[0]
    half_frame = FT // 2
    device_index = lax.axis_index("frame")
    stacked = jnp.stack((key_proj, value_proj))
    prev_frame_kv = shifted(stacked[:, :, half_frame:], "frame", 1)
    near_frames = shifted(stacked, "frame", 2)
    far_frames = shifted(stacked, "frame", 8)
    positions = jnp.arange(FT, dtype=jnp.int32)
    outputs = []
    for within in range(2):
        frame_id = 2 * device_index + within
        lower = within * half_frame
        upper = (within + 1) * half_frame
        own_kv = stacked[:, :, lower:upper]
        before_kv = prev_frame_kv if within == 0 else stacked[:, :, :half_frame]
        gathered_kv = jnp.concatenate(
            (own_kv, before_kv, near_frames[:, :, lower:upper], far_frames[:, :, lower:upper]), 2
        )
        gathered_kv = gathered_kv.reshape(2, local_heads, 4 * FT, HS)
        sources = (frame_id, frame_id - 1, frame_id - 4, frame_id - 16)
        key_valid = jnp.concatenate(
            [positions < frame_count(lengths, source) for source in sources], 0
        )
        frame_queries = query_proj[:, lower:upper].reshape(local_heads, FT, HS)
        outputs.append(
            attend(frame_queries, gathered_kv[0], gathered_kv[1], key_valid, local_heads)
        )
    attended = jnp.concatenate(outputs, 0)
    summed = lax.psum_scatter(
        jnp.dot(attended, out_weight, preferred_element_type=jnp.float32),
        "head",
        scatter_dimension=0,
        tiled=True,
    )
    return summed.astype(jnp.bfloat16)


def solution(mesh):
    return jax.shard_map(
        shards,
        mesh=mesh,
        in_specs=(
            P("head", "frame", None),
            P("head", "frame", None),
            P("head", "frame", None),
            P(),
            P("head", None),
        ),
        out_specs=P(("frame", "head"), None),
        check_vma=False,
    )
```

profile of v0, /device:TPU:5, one launch (start us, length us, event | category | flops | bytes accessed | tf_op | source)
XLA Modules:
  0.0 284.1 jit_solution(2804789728716470658)
XLA Ops:
  6.5 1.2 pad_maximum_fusion.2
  7.8 4.9 %collective-permute-start.1 = (bf16[2,1,1536,128]{3,2,1,0:T(8,128)(2,1)S(1)}, bf16[2,1,1536,128]{3,2,1,0:T(8,128)(2,1)S(1)}, u32[]{:S(2)}, u32[]{:S(2)}) collective-permute-start(bf16[2,1,1536,128]{3,2,1,0:T(8,128)(2,1)S(1)} %pad_maximum_fusion.2), channel_id=1, source_target_pairs={{0,32},{16,48},{32,64},{48,80},{64,96},{80,112},{96,128},{112,144}... | collective-permute-start | bytes 2359304 | tf_op jit(solution)/shard_map/ppermute | solution.py:15
  12.7 1.3 collective-permute-start.2
  14.0 1.3 fusion.43
  15.3 3.5 %collective-permute-start = (bf16[2,1,768,128]{3,2,1,0:T(8,128)(2,1)S(1)}, bf16[2,1,768,128]{3,2,1,0:T(8,128)(2,1)}, u32[]{:S(2)}, u32[]{:S(2)}) collective-permute-start(bf16[2,1,768,128]{3,2,1,0:T(8,128)(2,1)S(1)} %get-tuple-element.126), channel_id=1, source_target_pairs={{0,16},{16,32},{32,48},{48,64},{64,80},{80,96},{96,112},{112,128},... | collective-permute-start | bytes 1179656 | tf_op jit(solution)/shard_map/ppermute | solution.py:15
  18.8 1.7 fusion.60
  20.6 1.9 transpose_reshape_reshape.6
  22.4 0.9 transpose_reshape_reshape.7
  23.3 1.5 fusion.49
  24.8 0.6 iota_compare_fusion.6
  25.4 1.4 iota_compare_fusion
  26.8 1.2 iota_compare_fusion.2
  28.0 1.3 iota_compare_fusion.4
  29.3 0.6 pad_add_fusion
  29.9 6.9 %collective-permute-done.1 = bf16[2,1,1536,128]{3,2,1,0:T(8,128)(2,1)S(1)} collective-permute-done((bf16[2,1,1536,128]{3,2,1,0:T(8,128)(2,1)S(1)}, bf16[2,1,1536,128]{3,2,1,0:T(8,128)(2,1)S(1)}, u32[]{:S(2)}, u32[]{:S(2)}) %collective-permute-start.1) | collective-permute-done | bytes 786464 | tf_op jit(solution)/shard_map/ppermute | solution.py:15
  36.8 0.1 fusion.58
  36.9 13.3 %collective-permute-done.2 = bf16[2,1,1536,128]{3,2,1,0:T(8,128)(2,1)S(1)} collective-permute-done((bf16[2,1,1536,128]{3,2,1,0:T(8,128)(2,1)S(1)}, bf16[2,1,1536,128]{3,2,1,0:T(8,128)(2,1)S(1)}, u32[]{:S(2)}, u32[]{:S(2)}) %collective-permute-start.2) | collective-permute-done | bytes 786464 | tf_op jit(solution)/shard_map/ppermute | solution.py:15
  50.2 8.9 %collective-permute-done = bf16[2,1,768,128]{3,2,1,0:T(8,128)(2,1)} collective-permute-done((bf16[2,1,768,128]{3,2,1,0:T(8,128)(2,1)S(1)}, bf16[2,1,768,128]{3,2,1,0:T(8,128)(2,1)}, u32[]{:S(2)}, u32[]{:S(2)}) %collective-permute-start) | collective-permute-done | bytes 393248 | tf_op jit(solution)/shard_map/ppermute | solution.py:15
  59.1 1.2 pad_maximum_fusion
  60.2 1.4 fusion.56
  61.6 0.7 squeeze.15
  62.3 1.6 squeeze.16
  64.0 30.4 %while.20 = (s32[]{:T(128)}, bf16[3,512,64]{1,2,0:T(8,128)(2,1)S(1)}, pred[6144]{0:T(1024)(128)(4,1)S(1)}, bf16[3,1,512,64]{3,2,1,0:T(8,128)(2,1)}, bf16[1,6144,...) while((s32[]{:T(128)}, bf16[3,512,64]{1,2,0:T(8,128)(2,1)S(1)}, ...), condition=%wide.region_7.8_spmd, body=%wide.region_4.7_spmd.sunk | while | flops 849378304 | bytes 43479660 | solution.py:45
  64.0 3.1 %fusion.71 = (f32[512]{0:T(512)S(1)}, f32[512,6144]{1,0:T(8,128)S(1)}) fusion(pred[6144]{0:T(1024)(128)(4,1)S(1)} %get-tuple-element.261, bf16[1,6144,64]{2,1,0:T(8,128)(2,1)S(1)} %get-tuple-element.263, bf16[3,1,512,64]{3,2,1,0:T(8,128)(2,1)} %get-tuple-element.262, s32[]{:T(128)} %get-tuple-element.252), kind=kOutput, calls=%fused_computation.3.clone.1 | convolution fusion | flops 412089856 | bytes 13509120 | tf_op jit(solution)/shard_map/while/body/eval_jaxpr/hqd,hkd->hqk/dot_general | solution.py:33
  67.1 3.2 %fusion.72 = f32[512]{0:T(512)S(1)} fusion(f32[512,6144]{1,0:T(8,128)S(1)} %get-tuple-element.214, f32[512]{0:T(512)S(1)} %get-tuple-element.215, pred[6144]{0:T(1024)(128)(4,1)S(1)} %get-tuple-element.261), kind=kLoop, calls=%fused_computation.4.clone.1 | loop fusion | flops 15728128 | bytes 12593152 | tf_op jit(solution)/shard_map/while/body/eval_jaxpr/reduce_sum | solution.py:39
  70.4 3.8 %fusion.73 = bf16[3,512,64]{1,2,0:T(8,128)(2,1)S(1)} fusion(bf16[3,512,64]{1,2,0:T(8,128)(2,1)S(1)} %get-tuple-element.253, s32[]{:T(128)} %get-tuple-element.252, bf16[1,6144,64]{2,1,0:T(8,128)(2,1)S(1)} %copy-done.5, f32[512,6144]{1,0:T(8,128)S(1)} %get-tuple-element.214, f32[512]{0:T(512)S(1)} %fusion.72, f32[512]{0:T(512)S(1)} %get-tuple-element.215, ...), kind=kOutput, calls=%fused_computation.11.clone.1 | convolution fusion | flops 421560320 | bytes 14231556 | tf_op jit(solution)/shard_map/while/body/eval_jaxpr/hqk,hkd->qhd/dot_general | solution.py:40
  74.2 3.1 %fusion.71 = (f32[512]{0:T(512)S(1)}, f32[512,6144]{1,0:T(8,128)S(1)}) fusion(pred[6144]{0:T(1024)(128)(4,1)S(1)} %get-tuple-element.261, bf16[1,6144,64]{2,1,0:T(8,128)(2,1)S(1)} %get-tuple-element.263, bf16[3,1,512,64]{3,2,1,0:T(8,128)(2,1)} %get-tuple-element.262, s32[]{:T(128)} %get-tuple-element.252), kind=kOutput, calls=%fused_computation.3.clone.1 | convolution fusion | flops 412089856 | bytes 13509120 | tf_op jit(solution)/shard_map/while/body/eval_jaxpr/hqd,hkd->hqk/dot_general | solution.py:33
  77.3 3.2 %fusion.72 = f32[512]{0:T(512)S(1)} fusion(f32[512,6144]{1,0:T(8,128)S(1)} %get-tuple-element.214, f32[512]{0:T(512)S(1)} %get-tuple-element.215, pred[6144]{0:T(1024)(128)(4,1)S(1)} %get-tuple-element.261), kind=kLoop, calls=%fused_computation.4.clone.1 | loop fusion | flops 15728128 | bytes 12593152 | tf_op jit(solution)/shard_map/while/body/eval_jaxpr/reduce_sum | solution.py:39
  80.5 3.8 %fusion.73 = bf16[3,512,64]{1,2,0:T(8,128)(2,1)S(1)} fusion(bf16[3,512,64]{1,2,0:T(8,128)(2,1)S(1)} %get-tuple-element.253, s32[]{:T(128)} %get-tuple-element.252, bf16[1,6144,64]{2,1,0:T(8,128)(2,1)S(1)} %copy-done.5, f32[512,6144]{1,0:T(8,128)S(1)} %get-tuple-element.214, f32[512]{0:T(512)S(1)} %fusion.72, f32[512]{0:T(512)S(1)} %get-tuple-element.215, ...), kind=kOutput, calls=%fused_computation.11.clone.1 | convolution fusion | flops 421560320 | bytes 14231556 | tf_op jit(solution)/shard_map/while/body/eval_jaxpr/hqk,hkd->qhd/dot_general | solution.py:40
  84.3 3.1 %fusion.71 = (f32[512]{0:T(512)S(1)}, f32[512,6144]{1,0:T(8,128)S(1)}) fusion(pred[6144]{0:T(1024)(128)(4,1)S(1)} %get-tuple-element.261, bf16[1,6144,64]{2,1,0:T(8,128)(2,1)S(1)} %get-tuple-element.263, bf16[3,1,512,64]{3,2,1,0:T(8,128)(2,1)} %get-tuple-element.262, s32[]{:T(128)} %get-tuple-element.252), kind=kOutput, calls=%fused_computation.3.clone.1 | convolution fusion | flops 412089856 | bytes 13509120 | tf_op jit(solution)/shard_map/while/body/eval_jaxpr/hqd,hkd->hqk/dot_general | solution.py:33
  87.4 3.2 %fusion.72 = f32[512]{0:T(512)S(1)} fusion(f32[512,6144]{1,0:T(8,128)S(1)} %get-tuple-element.214, f32[512]{0:T(512)S(1)} %get-tuple-element.215, pred[6144]{0:T(1024)(128)(4,1)S(1)} %get-tuple-element.261), kind=kLoop, calls=%fused_computation.4.clone.1 | loop fusion | flops 15728128 | bytes 12593152 | tf_op jit(solution)/shard_map/while/body/eval_jaxpr/reduce_sum | solution.py:39
  90.6 3.8 %fusion.73 = bf16[3,512,64]{1,2,0:T(8,128)(2,1)S(1)} fusion(bf16[3,512,64]{1,2,0:T(8,128)(2,1)S(1)} %get-tuple-element.253, s32[]{:T(128)} %get-tuple-element.252, bf16[1,6144,64]{2,1,0:T(8,128)(2,1)S(1)} %copy-done.5, f32[512,6144]{1,0:T(8,128)S(1)} %get-tuple-element.214, f32[512]{0:T(512)S(1)} %fusion.72, f32[512]{0:T(512)S(1)} %get-tuple-element.215, ...), kind=kOutput, calls=%fused_computation.11.clone.1 | convolution fusion | flops 421560320 | bytes 14231556 | tf_op jit(solution)/shard_map/while/body/eval_jaxpr/hqk,hkd->qhd/dot_general | solution.py:40
  94.4 0.7 copy.10
  95.1 0.7 squeeze.17
  95.8 1.6 squeeze.18
  97.5 30.6 %while.21 = (s32[]{:T(128)}, bf16[3,512,64]{1,2,0:T(8,128)(2,1)S(1)}, pred[6144]{0:T(1024)(128)(4,1)S(1)}, bf16[3,1,512,64]{3,2,1,0:T(8,128)(2,1)}, bf16[1,6144,...) while((s32[]{:T(128)}, bf16[3,512,64]{1,2,0:T(8,128)(2,1)S(1)}, ...), condition=%wide.region_14.15_spmd, body=%wide.region_11.14_spmd.sunk | while | flops 849378304 | bytes 43479660 | solution.py:45
  97.7 3.1 %fusion.75 = (f32[512]{0:T(512)S(1)}, f32[512,6144]{1,0:T(8,128)S(1)}) fusion(pred[6144]{0:T(1024)(128)(4,1)S(1)} %get-tuple-element.240, bf16[1,6144,64]{2,1,0:T(8,128)(2,1)S(1)} %get-tuple-element.242, bf16[3,1,512,64]{3,2,1,0:T(8,128)(2,1)} %get-tuple-element.241, s32[]{:T(128)} %get-tuple-element.231), kind=kOutput, calls=%fused_computation.21.clone.1 | convolution fusion | flops 412089856 | bytes 13509120 | tf_op jit(solution)/shard_map/while/body/eval_jaxpr/hqd,hkd->hqk/dot_general | solution.py:33
  100.8 3.2 %fusion.76 = f32[512]{0:T(512)S(1)} fusion(f32[512,6144]{1,0:T(8,128)S(1)} %get-tuple-element.222, f32[512]{0:T(512)S(1)} %get-tuple-element.223, pred[6144]{0:T(1024)(128)(4,1)S(1)} %get-tuple-element.240), kind=kLoop, calls=%fused_computation.22.clone.1 | loop fusion | flops 15728128 | bytes 12593152 | tf_op jit(solution)/shard_map/while/body/eval_jaxpr/reduce_sum | solution.py:39
  104.1 3.8 %fusion.77 = bf16[3,512,64]{1,2,0:T(8,128)(2,1)S(1)} fusion(bf16[3,512,64]{1,2,0:T(8,128)(2,1)S(1)} %get-tuple-element.232, s32[]{:T(128)} %get-tuple-element.231, bf16[1,6144,64]{2,1,0:T(8,128)(2,1)S(1)} %copy-done.4, f32[512,6144]{1,0:T(8,128)S(1)} %get-tuple-element.222, f32[512]{0:T(512)S(1)} %fusion.76, f32[512]{0:T(512)S(1)} %get-tuple-element.223, ...), kind=kOutput, calls=%fused_computation.29.clone.1 | convolution fusion | flops 421560320 | bytes 14231556 | tf_op jit(solution)/shard_map/while/body/eval_jaxpr/hqk,hkd->qhd/dot_general | solution.py:40
  107.9 3.1 %fusion.75 = (f32[512]{0:T(512)S(1)}, f32[512,6144]{1,0:T(8,128)S(1)}) fusion(pred[6144]{0:T(1024)(128)(4,1)S(1)} %get-tuple-element.240, bf16[1,6144,64]{2,1,0:T(8,128)(2,1)S(1)} %get-tuple-element.242, bf16[3,1,512,64]{3,2,1,0:T(8,128)(2,1)} %get-tuple-element.241, s32[]{:T(128)} %get-tuple-element.231), kind=kOutput, calls=%fused_computation.21.clone.1 | convolution fusion | flops 412089856 | bytes 13509120 | tf_op jit(solution)/shard_map/while/body/eval_jaxpr/hqd,hkd->hqk/dot_general | solution.py:33
  111.0 3.2 %fusion.76 = f32[512]{0:T(512)S(1)} fusion(f32[512,6144]{1,0:T(8,128)S(1)} %get-tuple-element.222, f32[512]{0:T(512)S(1)} %get-tuple-element.223, pred[6144]{0:T(1024)(128)(4,1)S(1)} %get-tuple-element.240), kind=kLoop, calls=%fused_computation.22.clone.1 | loop fusion | flops 15728128 | bytes 12593152 | tf_op jit(solution)/shard_map/while/body/eval_jaxpr/reduce_sum | solution.py:39
  114.2 3.8 %fusion.77 = bf16[3,512,64]{1,2,0:T(8,128)(2,1)S(1)} fusion(bf16[3,512,64]{1,2,0:T(8,128)(2,1)S(1)} %get-tuple-element.232, s32[]{:T(128)} %get-tuple-element.231, bf16[1,6144,64]{2,1,0:T(8,128)(2,1)S(1)} %copy-done.4, f32[512,6144]{1,0:T(8,128)S(1)} %get-tuple-element.222, f32[512]{0:T(512)S(1)} %fusion.76, f32[512]{0:T(512)S(1)} %get-tuple-element.223, ...), kind=kOutput, calls=%fused_computation.29.clone.1 | convolution fusion | flops 421560320 | bytes 14231556 | tf_op jit(solution)/shard_map/while/body/eval_jaxpr/hqk,hkd->qhd/dot_general | solution.py:40
  118.0 3.1 %fusion.75 = (f32[512]{0:T(512)S(1)}, f32[512,6144]{1,0:T(8,128)S(1)}) fusion(pred[6144]{0:T(1024)(128)(4,1)S(1)} %get-tuple-element.240, bf16[1,6144,64]{2,1,0:T(8,128)(2,1)S(1)} %get-tuple-element.242, bf16[3,1,512,64]{3,2,1,0:T(8,128)(2,1)} %get-tuple-element.241, s32[]{:T(128)} %get-tuple-element.231), kind=kOutput, calls=%fused_computation.21.clone.1 | convolution fusion | flops 412089856 | bytes 13509120 | tf_op jit(solution)/shard_map/while/body/eval_jaxpr/hqd,hkd->hqk/dot_general | solution.py:33
  121.1 3.2 %fusion.76 = f32[512]{0:T(512)S(1)} fusion(f32[512,6144]{1,0:T(8,128)S(1)} %get-tuple-element.222, f32[512]{0:T(512)S(1)} %get-tuple-element.223, pred[6144]{0:T(1024)(128)(4,1)S(1)} %get-tuple-element.240), kind=kLoop, calls=%fused_computation.22.clone.1 | loop fusion | flops 15728128 | bytes 12593152 | tf_op jit(solution)/shard_map/while/body/eval_jaxpr/reduce_sum | solution.py:39
  124.3 3.8 %fusion.77 = bf16[3,512,64]{1,2,0:T(8,128)(2,1)S(1)} fusion(bf16[3,512,64]{1,2,0:T(8,128)(2,1)S(1)} %get-tuple-element.232, s32[]{:T(128)} %get-tuple-element.231, bf16[1,6144,64]{2,1,0:T(8,128)(2,1)S(1)} %copy-done.4, f32[512,6144]{1,0:T(8,128)S(1)} %get-tuple-element.222, f32[512]{0:T(512)S(1)} %fusion.76, f32[512]{0:T(512)S(1)} %get-tuple-element.223, ...), kind=kOutput, calls=%fused_computation.29.clone.1 | convolution fusion | flops 421560320 | bytes 14231556 | tf_op jit(solution)/shard_map/while/body/eval_jaxpr/hqk,hkd->qhd/dot_general | solution.py:40
  128.2 6.4 %fusion.44 = f32[3072,1024]{1,0:T(8,128)} fusion(bf16[64,1024]{1,0:T(8,128)(2,1)S(1)} %copy-done, bf16[1536,64]{0,1:T(8,128)(2,1)S(1)} %bitcast.98, bf16[1536,64]{0,1:T(8,128)(2,1)S(1)} %bitcast.97), kind=kOutput, calls=%fused_computation.45 | convolution fusion | flops 403439616 | bytes 13107200 | tf_op jit(solution)/shard_map/dot_general | solution.py:78
  134.6 140.7 %reduce-scatter.2.cloned.1.call-done = f32[192,1024]{1,0:T(8,128)} async-done(((f32[3072,1024]{1,0:T(8,128)}), f32[192,1024]{1,0:T(8,128)}) %reduce-scatter.2.cloned.1.call-update) | async-done | bytes 786448 | tf_op jit(solution)/shard_map/reduce_scatter | solution.py:77
  275.3 1.9 convert_element_type.35
  (28 shorter events, 0.2 us)
Async XLA Ops:
  6.5 121.6 %copy-start = (bf16[64,1024]{1,0:T(8,128)(2,1)S(1)}, bf16[64,1024]{1,0:T(8,128)(2,1)}, u32[]{:S(2)}) copy-start(bf16[64,1024]{1,0:T(8,128)(2,1)} %param.13) | copy-start | bytes 393220
  6.5 268.7 %reduce-scatter.2.cloned.1.call-start = ((), (), s32[]{:S(2)}) async-start(), calls=%async_computation.1 | async-start | bytes 13369344 | tf_op jit(solution)/shard_map/reduce_scatter | solution.py:77
  7.8 29.0 %collective-permute-start.1 = (bf16[2,1,1536,128]{3,2,1,0:T(8,128)(2,1)S(1)}, bf16[2,1,1536,128]{3,2,1,0:T(8,128)(2,1)S(1)}, u32[]{:S(2)}, u32[]{:S(2)}) collective-permute-start(bf16[2,1,1536,128]{3,2,1,0:T(8,128)(2,1)S(1)} %pad_maximum_fusion.2), channel_id=1, source_target_pairs={{0,32},{16,48},{32,64},{48,80},{64,96},{80,112},{96,128},{112,144}... | collective-permute-start | bytes 2359304 | tf_op jit(solution)/shard_map/ppermute | solution.py:15
  12.7 37.5 %collective-permute-start.2 = (bf16[2,1,1536,128]{3,2,1,0:T(8,128)(2,1)S(1)}, bf16[2,1,1536,128]{3,2,1,0:T(8,128)(2,1)S(1)}, u32[]{:S(2)}, u32[]{:S(2)}) collective-permute-start(bf16[2,1,1536,128]{3,2,1,0:T(8,128)(2,1)S(1)} %pad_maximum_fusion.2), channel_id=1, source_target_pairs={{0,128},{16,144},{32,160},{48,176},{64,192},{80,208},{96,224},{112... | collective-permute-start | bytes 2359304 | tf_op jit(solution)/shard_map/ppermute | solution.py:15
  15.3 43.8 %collective-permute-start = (bf16[2,1,768,128]{3,2,1,0:T(8,128)(2,1)S(1)}, bf16[2,1,768,128]{3,2,1,0:T(8,128)(2,1)}, u32[]{:S(2)}, u32[]{:S(2)}) collective-permute-start(bf16[2,1,768,128]{3,2,1,0:T(8,128)(2,1)S(1)} %get-tuple-element.126), channel_id=1, source_target_pairs={{0,16},{16,32},{32,48},{48,64},{64,80},{80,96},{96,112},{112,128},... | collective-permute-start | bytes 1179656 | tf_op jit(solution)/shard_map/ppermute | solution.py:15
  64.0 31.2 %copy-start.2 = (bf16[1,1,3072,128]{3,2,1,0:T(8,128)(2,1)S(1)}, bf16[1,1,3072,128]{3,2,1,0:T(8,128)(2,1)}, u32[]{:S(2)}) copy-start(bf16[1,1,3072,128]{3,2,1,0:T(8,128)(2,1)} %get-tuple-element.140) | copy-start | bytes 2359300
  64.0 31.9 %copy-start.1 = (bf16[1,1,3072,128]{3,2,1,0:T(8,128)(2,1)S(1)}, bf16[1,1,3072,128]{3,2,1,0:T(8,128)(2,1)}, u32[]{:S(2)}) copy-start(bf16[1,1,3072,128]{3,2,1,0:T(8,128)(2,1)} %get-tuple-element.141) | copy-start | bytes 2359300
  64.0 33.5 %copy-start.3 = (pred[6144]{0:T(1024)(128)(4,1)S(1)}, pred[6144]{0:T(1024)(128)(4,1)}, u32[]{:S(2)}) copy-start(pred[6144]{0:T(1024)(128)(4,1)} %get-tuple-element.226) | copy-start | bytes 18436
  64.0 6.4 %copy-start.5 = (bf16[1,6144,64]{2,1,0:T(8,128)(2,1)S(1)}, bf16[1,6144,64]{2,1,0:T(8,128)(2,1)}, u32[]{:S(2)}) copy-start(bf16[1,6144,64]{2,1,0:T(8,128)(2,1)} %get-tuple-element.264) | copy-start | bytes 2359300 | tf_op jit(solution)/shard_map/while
  74.2 6.3 %copy-start.5 = (bf16[1,6144,64]{2,1,0:T(8,128)(2,1)S(1)}, bf16[1,6144,64]{2,1,0:T(8,128)(2,1)}, u32[]{:S(2)}) copy-start(bf16[1,6144,64]{2,1,0:T(8,128)(2,1)} %get-tuple-element.264) | copy-start | bytes 2359300 | tf_op jit(solution)/shard_map/while
  84.3 6.3 %copy-start.5 = (bf16[1,6144,64]{2,1,0:T(8,128)(2,1)S(1)}, bf16[1,6144,64]{2,1,0:T(8,128)(2,1)}, u32[]{:S(2)}) copy-start(bf16[1,6144,64]{2,1,0:T(8,128)(2,1)} %get-tuple-element.264) | copy-start | bytes 2359300 | tf_op jit(solution)/shard_map/while
  97.5 30.6 %copy-start.6 = (bf16[3,8,8,512]{3,2,0,1:T(8,128)(2,1)S(1)}, bf16[3,8,8,512]{3,2,0,1:T(8,128)(2,1)}, u32[]{:S(2)}) copy-start(bf16[3,8,8,512]{3,2,0,1:T(8,128)(2,1)} %copy.10) | copy-start | bytes 589828
  97.7 6.3 %copy-start.4 = (bf16[1,6144,64]{2,1,0:T(8,128)(2,1)S(1)}, bf16[1,6144,64]{2,1,0:T(8,128)(2,1)}, u32[]{:S(2)}) copy-start(bf16[1,6144,64]{2,1,0:T(8,128)(2,1)} %get-tuple-element.243) | copy-start | bytes 2359300 | tf_op jit(solution)/shard_map/while
  107.8 6.3 %copy-start.4 = (bf16[1,6144,64]{2,1,0:T(8,128)(2,1)S(1)}, bf16[1,6144,64]{2,1,0:T(8,128)(2,1)}, u32[]{:S(2)}) copy-start(bf16[1,6144,64]{2,1,0:T(8,128)(2,1)} %get-tuple-element.243) | copy-start | bytes 2359300 | tf_op jit(solution)/shard_map/while
  118.0 6.3 %copy-start.4 = (bf16[1,6144,64]{2,1,0:T(8,128)(2,1)S(1)}, bf16[1,6144,64]{2,1,0:T(8,128)(2,1)}, u32[]{:S(2)}) copy-start(bf16[1,6144,64]{2,1,0:T(8,128)(2,1)} %get-tuple-element.243) | copy-start | bytes 2359300 | tf_op jit(solution)/shard_map/while
Sparse Core Ops, SparseCore 0:
  134.7 140.5 reduce-scatter.1
where the time goes:
time: 286 us; the launch traced here: 284 us
  waiting for transfers between devices  170 us (59%)
  matrix products  47.7 us (17%)
  other arithmetic  31.5 us (11%)
  between operations  13.6 us (5%)
  local copies, waits for them, and re-layouts  11.4 us (4%)
  starting transfers between devices  9.74 us (3%)
    reduce_scatter x1, waiting for transfers between devices, shards(): lax.psum_scatter(jnp.dot(attended, out_weight, preferred_element_type=jnp...  141 us
    ppermute x3, waiting for transfers between devices, shifted(): return lax.ppermute(x, axis, pairs)  29 us
    dot_general x6, matrix products, one_block(): jnp.einsum('hqk,hkd->qhd', weights, value_block, preferred_element_type=j...  22.6 us
    reduce_sum x6, other arithmetic, one_block(): jnp.sum(expon, axis=2, keepdims=True)  19.3 us
    dot_general x6, matrix products, one_block(): jnp.einsum('hqd,hkd->hqk', query_part, key_block, preferred_element_type=...  18.7 us
    ppermute x3, starting transfers between devices, shifted(): return lax.ppermute(x, axis, pairs)  9.74 us
    dot_general x1, matrix products, shards(): jnp.dot(attended, out_weight, preferred_element_type=jnp.float32)  6.4 us
  transfers between devices with their start and end apart: 4, of which 4 were waited for; matrix products, arithmetic and copies ran while one was open for 4% of the time, Pallas kernels for 0%

commit v1 on v0

v1 whole, which is shorter than its diff:
```python
import jax
import jax.numpy as jnp
from jax import lax
from jax.experimental import pallas as pl
from jax.experimental.pallas import tpu as pltpu
from jax.sharding import PartitionSpec as P

MESH = pl.DeviceIdType.MESH
BF = jnp.bfloat16
F32 = jnp.float32
HS = 64
PR = 768
KC = 256
NCH = PR // KC
SCALE = 1.4426950408889634 / 8.0
LOW = -1.0e30


def kernel(q_ref, k_ref, v_ref, len_ref, w_ref, o_ref,
           qraw, kprev, vprev, kfar, vfar, qt, ka, vt, s0, s1, m0, m1, acc,
           oout, oin, wbuf, att, abuf, xbuf,
           q_s, q_r, p_s, p_r, f_s, f_r, o_s, o_r, w_s, w_r, g_s, g_r, a_s, a_r):
    d = lax.axis_index("frame")
    h = lax.axis_index("head")
    hp = h // 2
    core = h % 2
    has_prev = d >= 1
    gives_prev = d <= 14
    has_near = d >= 2
    does_near = d <= 13
    has_far = d >= 8

    bar = pltpu.get_barrier_semaphore()
    for shift in (1, 2, 8):
        @pl.when(d >= shift)
        def _():
            pl.semaphore_signal(bar, inc=1, device_id={"frame": d - shift}, device_id_type=MESH)

        @pl.when(d + shift <= 15)
        def _():
            pl.semaphore_signal(bar, inc=1, device_id={"frame": d + shift}, device_id_type=MESH)
    for step in range(1, 16):
        pl.semaphore_signal(bar, inc=1, device_id={"head": (h + step) % 16}, device_id_type=MESH)
    one = lambda c: jnp.where(c, 1, 0)
    pl.semaphore_wait(bar, 16 + one(d >= 1) + one(d <= 14) + one(d >= 2) + one(d <= 13))

    def q_copy(w):
        rows = pl.ds(w * PR, PR)
        return pltpu.make_async_remote_copy(q_ref.at[rows], qraw.at[rows], q_s.at[w], q_r.at[w],
                                            device_id={"frame": d - 2}, device_id_type=MESH)

    def prev_copy(n):
        src, dst = ((k_ref, kprev), (v_ref, vprev))[n]
        return pltpu.make_async_remote_copy(src.at[pl.ds(PR, PR)], dst, p_s.at[n], p_r.at[n],
                                            device_id={"frame": d + 1}, device_id_type=MESH)

    def far_copy(n):
        src, dst = ((k_ref, kfar), (v_ref, vfar))[n]
        return pltpu.make_async_remote_copy(src, dst, f_s.at[n], f_r.at[n],
                                            device_id={"frame": d + 8}, device_id_type=MESH)

    def out_copy(w, par):
        lo, n = ((0, 64), (64, 80))[par]
        return pltpu.make_async_remote_copy(oout.at[w, pl.ds(lo, n)], oin.at[w, pl.ds(lo, n)],
                                            o_s.at[2 * w + par], o_r.at[2 * w + par],
                                            device_id={"frame": d + 2}, device_id_type=MESH)

    def w_rows(head):
        return pl.ds(pl.multiple_of(head * HS, HS), HS)

    def w_copy(step):
        return pltpu.make_async_remote_copy(w_ref, wbuf.at[w_rows(h)], w_s.at[step], w_r.at[hp],
                                            device_id={"head": ((hp + step) % 8) * 2 + core}, device_id_type=MESH)

    def w_wait(step):
        src = (hp + 8 - step) % 8
        return pltpu.make_async_remote_copy(w_ref, wbuf.at[w_rows(2 * src + core)], w_s.at[step], w_r.at[src],
                                            device_id={"head": 2 * src + core}, device_id_type=MESH)

    def g_own():
        return pltpu.make_async_remote_copy(w_ref, wbuf.at[w_rows(h)], g_s.at[hp], g_r.at[hp],
                                            device_id={"head": h + 1 - 2 * core}, device_id_type=MESH)

    def g_copy(step):
        src = (hp + 8 - step) % 8
        rows = w_rows(2 * src + core)
        return pltpu.make_async_remote_copy(wbuf.at[rows], wbuf.at[rows], g_s.at[src], g_r.at[src],
                                            device_id={"head": h + 1 - 2 * core}, device_id_type=MESH)

    def g_wait(src):
        rows = w_rows(2 * src + 1 - core)
        return pltpu.make_async_remote_copy(wbuf.at[rows], wbuf.at[rows], g_s.at[src], g_r.at[src],
                                            device_id={"head": h + 1 - 2 * core}, device_id_type=MESH)

    def a_copy(j):
        return pltpu.make_async_remote_copy(att.at[pl.ds(96 * j, 96)], abuf.at[h], a_s.at[j], a_r.at[h],
                                            device_id={"head": j}, device_id_type=MESH)

    def a_wait(j):
        return pltpu.make_async_remote_copy(att.at[pl.ds(96 * j, 96)], abuf.at[j], a_s.at[j], a_r.at[j],
                                            device_id={"head": j}, device_id_type=MESH)

    @pl.when(has_near)
    def _():
        q_copy(0).start()
        q_copy(1).start()

    @pl.when(gives_prev)
    def _():
        prev_copy(0).start()
        prev_copy(1).start()

    @pl.when(d <= 7)
    def _():
        far_copy(0).start()
        far_copy(1).start()

    for step in range(1, 8):
        w_copy(step).start()
    g_own().start()
    wbuf[w_rows(h), :] = w_ref[...]

    lane = lax.broadcasted_iota(jnp.int32, (PR, 128), 1)
    row = lax.broadcasted_iota(jnp.int32, (PR, 128), 0)
    position = 2 * row + jnp.where(lane >= 64, 1, 0)
    column = lax.broadcasted_iota(jnp.int32, (16, PR), 1)

    def prep_kv(slot, keys, values, frame):
        count = len_ref[jnp.maximum(frame, 0)]
        valid = position < count
        first = jnp.broadcast_to(keys[0:1, :].astype(F32), (PR, 128))
        ka[slot] = jnp.where(valid, keys.astype(F32), first).astype(BF)
        turned = jnp.where(valid, values.astype(F32), 0.0).astype(BF).T
        for p in range(2):
            vt[slot, p, 0:64] = turned[64 * p:64 * p + 64]
            vt[slot, p, 64:80] = jnp.where(2 * column + p < count, 1.0, 0.0).astype(BF)

    def prep_q(slot, queries):
        x = queries.astype(F32) * SCALE
        hi = x.astype(BF)
        low = (x - hi.astype(F32))
        for n, part in enumerate((hi.astype(F32), low)):
            swapped = pltpu.roll(part, 64, 1)
            rows = slice(128 * n, 128 * n + 128)
            qt[slot, 0, 0, rows] = jnp.where(lane < 64, part, 0.0).astype(BF).T
            qt[slot, 0, 1, rows] = jnp.where(lane < 64, 0.0, swapped).astype(BF).T
            qt[slot, 1, 0, rows] = jnp.where(lane < 64, swapped, 0.0).astype(BF).T
            qt[slot, 1, 1, rows] = jnp.where(lane < 64, 0.0, part).astype(BF).T

    for w in range(2):
        prep_q(w, q_ref[pl.ds(w * PR, PR), :])
        prep_kv(w, k_ref[pl.ds(w * PR, PR), :], v_ref[pl.ds(w * PR, PR), :], 2 * d + w)
    for t in range(4):
        for par in range(2):
            acc[t, par, 0:80] = jnp.zeros((80, PR), F32)
            acc[t, par, 80:88] = jnp.full((8, PR), LOW, F32)

    count = jnp.where(has_far, jnp.where(does_near, 8, 6), jnp.where(has_prev, 6, 5))

    def pair_of(i):
        late = jnp.where(i == 3, 4, jnp.where(i == 4, 5, jnp.where(i == 5, 7, i)))
        early = jnp.where(i == 4, jnp.where(has_prev, 4, 6), jnp.where(i == 5, 6, i))
        return jnp.where(does_near, jnp.where(has_far, i, early), late)

    def slots(j):
        q = jnp.where(j == 3, 2, jnp.where(j == 6, 3, jnp.where((j == 1) | (j == 2) | (j == 7), 1, 0)))
        k = jnp.where(j == 4, 2, jnp.where(j == 5, 3, jnp.where(j == 7, 4, jnp.where((j == 1) | (j == 6), 1, 0))))
        return q, k

    chunks = [(c, p) for p in range(2) for c in range(NCH)]

    def score(q, k, par, dst, c, p, top):
        rows = slice((p * NCH + c) * KC, (p * NCH + c + 1) * KC)
        keys = ka[k, c * KC:(c + 1) * KC]
        sc = jnp.dot(jnp.concatenate([keys, keys], axis=1), qt[q, par, p], preferred_element_type=F32)
        dst[rows] = sc
        best = jnp.max(sc.reshape(KC // 8, 8, PR), axis=0)
        return best if top is None else jnp.maximum(top, best)

    def finish_top(top, dst):
        best = jnp.max(top, axis=0, keepdims=True).astype(BF).astype(F32)
        dst[...] = jnp.broadcast_to(best, (8, PR))

    def step(q, k, par, sb, mb, qn, kn, parn, sn, mn):
        m = mb[0:1]
        total, top = None, None
        for c, p in chunks:
            top = score(qn, kn, parn, sn, c, p, top)
            rows = slice((p * NCH + c) * KC, (p * NCH + c + 1) * KC)
            e = jnp.exp2(sb[rows] - m).astype(BF)
            part = jnp.dot(vt[k, p, :, c * KC:(c + 1) * KC], e, preferred_element_type=F32)
            total = part if total is None else total + part
        finish_top(top, mn)
        old = acc[q, par, 80:81]
        new = jnp.maximum(old, m)
        acc[q, par, 0:80] = acc[q, par, 0:80] * jnp.exp2(old - new) + total * jnp.exp2(m - new)
        acc[q, par, 80:88] = jnp.broadcast_to(new, (8, PR))

    def put_near(w, par):
        oout[w, 64 * par:64 * par + 64] = acc[2 + w, par, 0:64].astype(BF)

    def put_stats(w):
        parts = []
        for par in range(2):
            l = acc[2 + w, par, 64:65]
            hi = l.astype(BF).astype(F32)
            parts += [hi, l - hi, acc[2 + w, par, 80:81]]
        pad = jnp.zeros((10, PR), F32)
        oout[w, 128:144] = jnp.concatenate(parts + [pad], axis=0).astype(BF)

    top = None
    for c, p in chunks:
        top = score(0, 0, 0, s0, c, p, top)
    finish_top(top, m0)

    def body(i, _):
        j = pair_of(i)
        nxt = pair_of(jnp.minimum(i + 1, count - 1))
        fresh = i + 1 < count
        for w, at in ((0, 3), (1, 6)):
            @pl.when(fresh & (nxt == at))
            def _():
                q_copy(w).wait_recv()
                prep_q(2 + w, qraw[pl.ds(w * PR, PR), :])

        @pl.when(fresh & (nxt == 4))
        def _():
            prev_copy(0).wait_recv()
            prev_copy(1).wait_recv()
            prep_kv(2, kprev[...], vprev[...], 2 * d - 1)

        @pl.when(fresh & (nxt == 5))
        def _():
            far_copy(0).wait_recv()
            far_copy(1).wait_recv()
            prep_kv(3, kfar[pl.ds(0, PR), :], vfar[pl.ds(0, PR), :], 2 * d - 16)
            prep_kv(4, kfar[pl.ds(PR, PR), :], vfar[pl.ds(PR, PR), :], 2 * d - 15)

        q, k = slots(j)
        qn, kn = slots(nxt)
        step(q, k, 0, s0, m0, q, k, 1, s1, m1)
        for w, at in ((0, 3), (1, 6)):
            @pl.when(j == at)
            def _():
                put_near(w, 0)
                out_copy(w, 0).start()
        step(q, k, 1, s1, m1, qn, kn, 0, s0, m0)
        for w, at in ((0, 3), (1, 6)):
            @pl.when(j == at)
            def _():
                put_near(w, 1)
                put_stats(w)
                out_copy(w, 1).start()

        @pl.when(i == 3)
        def _():
            for s in range(1, 8):
                w_wait(s).wait_recv()
                g_copy(s).start()
        return 0

    lax.fori_loop(0, count, body, 0)

    for w in range(2):
        @pl.when(has_near)
        def _():
            out_copy(w, 0).wait_recv()
            out_copy(w, 1).wait_recv()
            stats = oin[w, 128:144].astype(F32)
            for par in range(2):
                l = stats[3 * par:3 * par + 1] + stats[3 * par + 1:3 * par + 2]
                m = stats[3 * par + 2:3 * par + 3]
                part = oin[w, 64 * par:64 * par + 64].astype(F32)
                old = acc[w, par, 80:81]
                new = jnp.maximum(old, m)
                fo, fn = jnp.exp2(old - new), jnp.exp2(m - new)
                acc[w, par, 0:64] = acc[w, par, 0:64] * fo + part * fn
                acc[w, par, 64:65] = acc[w, par, 64:65] * fo + l * fn
        halves = []
        for par in range(2):
            halves.append((acc[w, par, 0:64] * (1.0 / acc[w, par, 64:65])).astype(BF))
        att[pl.ds(w * PR, PR), :] = jnp.concatenate(halves, axis=0).T
        for j in range(8 * w, 8 * w + 8):
            @pl.when(h == j)
            def _():
                abuf[j] = att[96 * j:96 * j + 96, :]

            @pl.when(h != j)
            def _():
                a_copy(j).start()

    for src in range(8):
        g_wait(src).wait_recv()
    low_half = lax.broadcasted_iota(jnp.int32, (96, 128), 1) < 64
    for n in range(8):
        for j in (2 * n, 2 * n + 1):
            @pl.when(h != j)
            def _():
                a_wait(j).wait_recv()
        a = abuf[2 * n].astype(F32)
        b = abuf[2 * n + 1].astype(F32)
        xbuf[0:96, 128 * n:128 * n + 128] = jnp.where(low_half, a, pltpu.roll(b, 64, 1)).astype(BF)
        xbuf[96:192, 128 * n:128 * n + 128] = jnp.where(low_half, pltpu.roll(a, 64, 1), b).astype(BF)
    out = jnp.dot(xbuf[...], wbuf[...], preferred_element_type=F32).astype(BF)
    o_ref[:, 0:1024] = out[0:96]
    o_ref[:, 1024:2048] = out[96:192]

    @pl.when(has_near)
    def _():
        q_copy(0).wait_send()
        q_copy(1).wait_send()

    @pl.when(gives_prev)
    def _():
        prev_copy(0).wait_send()
        prev_copy(1).wait_send()

    @pl.when(d <= 7)
    def _():
        far_copy(0).wait_send()
        far_copy(1).wait_send()

    @pl.when(does_near)
    def _():
        for w in range(2):
            for par in range(2):
                out_copy(w, par).wait_send()

    g_own().wait_send()
    for s in range(1, 8):
        w_copy(s).wait_send()
        g_copy(s).wait_send()
    for j in range(16):
        @pl.when(h != j)
        def _():
            a_copy(j).wait_send()


def shards(query_proj, key_proj, value_proj, lengths, out_weight):
    vmem = pl.BlockSpec(memory_space=pltpu.VMEM)
    smem = pl.BlockSpec(memory_space=pltpu.SMEM)
    dma = pltpu.SemaphoreType.DMA
    out = pl.pallas_call(
        kernel,
        out_shape=jax.ShapeDtypeStruct((96, 2048), BF),
        in_specs=[vmem, vmem, vmem, smem, vmem],
        out_specs=vmem,
        scratch_shapes=[
            pltpu.VMEM((2 * PR, 128), BF),
            pltpu.VMEM((PR, 128), BF),
            pltpu.VMEM((PR, 128), BF),
            pltpu.VMEM((2 * PR, 128), BF),
            pltpu.VMEM((2 * PR, 128), BF),
            pltpu.VMEM((4, 2, 2, 256, PR), BF),
            pltpu.VMEM((5, PR, 128), BF),
            pltpu.VMEM((5, 2, 80, PR), BF),
            pltpu.VMEM((2 * PR, PR), F32),
            pltpu.VMEM((2 * PR, PR), F32),
            pltpu.VMEM((8, PR), F32),
            pltpu.VMEM((8, PR), F32),
            pltpu.VMEM((4, 2, 88, PR), F32),
            pltpu.VMEM((2, 144, PR), BF),
            pltpu.VMEM((2, 144, PR), BF),
            pltpu.VMEM((1024, 1024), BF),
            pltpu.VMEM((2 * PR, 128), BF),
            pltpu.VMEM((16, 96, 128), BF),
            pltpu.VMEM((192, 1024), BF),
            dma((2,)), dma((2,)), dma((2,)), dma((2,)), dma((2,)), dma((2,)),
            dma((4,)), dma((4,)), dma((8,)), dma((8,)), dma((8,)), dma((8,)),
            dma((16,)), dma((16,)),
        ],
        compiler_params=pltpu.CompilerParams(collective_id=0, has_side_effects=True),
        name="fused",
    )(query_proj[0], key_proj[0], value_proj[0], lengths, out_weight)
    return out.reshape(192, 1024)


def solution(mesh):
    return jax.shard_map(
        shards,
        mesh=mesh,
        in_specs=(
            P("head", "frame", None),
            P("head", "frame", None),
            P("head", "frame", None),
            P(),
            P("head", None),
        ),
        out_specs=P(("frame", "head"), None),
        check_vma=False,
    )
```

time: 286 us -> 67.8 us (0.24)
  the two profiles are of different devices: /device:TPU:5 before, /device:TPU:89 now
where the time goes in v1:
time: 67.8 us; the launch traced here: 67.7 us
  Pallas kernels  65.8 us (97%)
  local copies, waits for them, and re-layouts  1.87 us (3%)
    pallas_call x1, Pallas kernels, shards(): pl.pallas_call(kernel, out_shape=jax.ShapeDtypeStruct((96, 2048), BF), in...  65.8 us
    reshape x1, local copies, waits for them, and re-layouts, shards(): return out.reshape(192, 1024)  1.87 us

profile of v1, /device:TPU:89, one launch (start us, length us, event | category | flops | bytes accessed | tf_op | source)
XLA Modules:
  0.0 67.7 jit_solution(12667217364538649586)
XLA Ops:
  0.0 65.8 %fused.1 = bf16[96,2048]{1,0:T(8,128)(2,1)} custom-call(bf16[1536,128]{1,0:T(8,128)(2,1)} %bitcast.3, bf16[1536,128]{1,0:T(8,128)(2,1)} %bitcast.4, bf16[1536,128]{1,0:T(8,128)(2,1)} %bitcast.5, s32[32]{0:T(128)} %len_ref.1, bf16[64,1024]{1,0:T(8,128)(2,1)} %w_ref.1), custom_call_target="tpu_custom_call" | custom-call | tf_op jit(solution)/shard_map/fused/pallas_call | solution.py:343
  65.8 1.9 %reshape.3 = bf16[192,1024]{1,0:T(8,128)(2,1)} reshape(bf16[96,2048]{1,0:T(8,128)(2,1)} %fused.1) | data formatting | bytes 786432 | tf_op jit(solution)/shard_map/reshape | solution.py:375

commit v2 on v1

--- a/solution.py
+++ b/solution.py
@@ -17,18 +17,35 @@
 
 
 def kernel(q_ref, k_ref, v_ref, len_ref, w_ref, o_ref,
-           qraw, kprev, vprev, kfar, vfar, qt, ka, vt, s0, s1, m0, m1, acc,
+           qraw, kprev, vprev, knear, vnear, kfar, vfar, qt, ka, vt, s0, s1, m0, m1, acc,
            oout, oin, wbuf, att, abuf, xbuf,
-           q_s, q_r, p_s, p_r, f_s, f_r, o_s, o_r, w_s, w_r, g_s, g_r, a_s, a_r):
+           q_s, q_r, p_s, p_r, n_s, n_r, f_s, f_r, o_s, o_r, w_s, w_r, g_s, g_r, a_s, a_r):
     d = lax.axis_index("frame")
     h = lax.axis_index("head")
     hp = h // 2
     core = h % 2
+    side = hp % 2
+    line = hp // 2
+    does = (d <= 13, (d <= 7) & (d != 6), d == 0, d == 6)
+    gets = (d >= 2, (d >= 8) & (d != 14), d == 8, d == 8)
+    away = (2, 8, 8, 2)
+    place = (0, 1, 2, 2)
     has_prev = d >= 1
     gives_prev = d <= 14
-    has_near = d >= 2
-    does_near = d <= 13
-    has_far = d >= 8
+    has_relay = (d >= 2) & (d != 8)
+    gives_relay = (d >= 1) & (d <= 14) & (d != 7)
+    has_far = (d >= 9, d == 14)
+    gives_far = ((d >= 1) & (d <= 7), d == 6)
+
+    def digits(values):
+        return sum(v << (4 * n) for n, v in enumerate(values))
+
+    order = jnp.where(d <= 7, digits((0, 1, 2, 3, 4, 7, 6)), digits((0, 1, 2, 3, 4, 5, 6)))
+    order = jnp.where(d == 0, digits((0, 1, 2, 3, 7, 9)), order)
+    order = jnp.where(d == 6, digits((0, 1, 2, 3, 9, 4, 6)), order)
+    order = jnp.where(d == 14, digits((0, 1, 2, 4, 5, 8, 6)), order)
+    order = jnp.where(d == 15, digits((0, 1, 2, 4, 5, 6)), order)
+    count = jnp.where((d <= 1) | (d == 15), 6, jnp.where(d == 8, 5, 7))
 
     bar = pltpu.get_barrier_semaphore()
     for shift in (1, 2, 8):
@@ -44,36 +61,47 @@
     one = lambda c: jnp.where(c, 1, 0)
     pl.semaphore_wait(bar, 16 + one(d >= 1) + one(d <= 14) + one(d >= 2) + one(d <= 13))
 
-    def q_copy(w):
-        rows = pl.ds(w * PR, PR)
-        return pltpu.make_async_remote_copy(q_ref.at[rows], qraw.at[rows], q_s.at[w], q_r.at[w],
-                                            device_id={"frame": d - 2}, device_id_type=MESH)
+    def q_copy(g):
+        return pltpu.make_async_remote_copy(q_ref.at[pl.ds((0, 1, 0, 1)[g] * PR, PR)], qraw.at[place[g]], q_s.at[g], q_r.at[g],
+                                            device_id={"frame": d - away[g]}, device_id_type=MESH)
 
     def prev_copy(n):
         src, dst = ((k_ref, kprev), (v_ref, vprev))[n]
         return pltpu.make_async_remote_copy(src.at[pl.ds(PR, PR)], dst, p_s.at[n], p_r.at[n],
                                             device_id={"frame": d + 1}, device_id_type=MESH)
 
-    def far_copy(n):
+    def relay_copy(n):
+        src, dst = ((kprev, knear), (vprev, vnear))[n]
+        return pltpu.make_async_remote_copy(src, dst, n_s.at[n], n_r.at[n],
+                                            device_id={"frame": d + 1}, device_id_type=MESH)
+
+    def far_copy(w, n):
         src, dst = ((k_ref, kfar), (v_ref, vfar))[n]
-        return pltpu.make_async_remote_copy(src, dst, f_s.at[n], f_r.at[n],
+        return pltpu.make_async_remote_copy(src.at[pl.ds(w * PR, PR)], dst.at[w], f_s.at[2 * w + n], f_r.at[2 * w + n],
                                             device_id={"frame": d + 8}, device_id_type=MESH)
 
-    def out_copy(w, par):
+    def out_copy(g, par):
         lo, n = ((0, 64), (64, 80))[par]
-        return pltpu.make_async_remote_copy(oout.at[w, pl.ds(lo, n)], oin.at[w, pl.ds(lo, n)],
-                                            o_s.at[2 * w + par], o_r.at[2 * w + par],
-                                            device_id={"frame": d + 2}, device_id_type=MESH)
+        return pltpu.make_async_remote_copy(oout.at[place[g], pl.ds(lo, n)], oin.at[g, pl.ds(lo, n)],
+                                            o_s.at[2 * g + par], o_r.at[2 * g + par],
+                                            device_id={"frame": d + away[g]}, device_id_type=MESH)
 
     def w_rows(head):
         return pl.ds(pl.multiple_of(head * HS, HS), HS)
 
     def w_copy(step):
-        return pltpu.make_async_remote_copy(w_ref, wbuf.at[w_rows(h)], w_s.at[step], w_r.at[hp],
-                                            device_id={"head": ((hp + step) % 8) * 2 + core}, device_id_type=MESH)
+        own = step < 4
+        shard = hp if own else 2 * line + 1 - side
+        to = 2 * line + 1 - side if step == 0 else 2 * ((line + (step if own else step - 3)) % 4) + side
+        rows = w_rows(2 * shard + core)
+        return pltpu.make_async_remote_copy(w_ref if own else wbuf.at[rows], wbuf.at[rows], w_s.at[step], w_r.at[shard],
+                                            device_id={"head": 2 * to + core}, device_id_type=MESH)
+
+    def shard_of(step):
+        return 2 * line + 1 - side if step == 0 else (hp + 2 * step) % 8 if step < 4 else 2 * ((line + step - 3) % 4) + 1 - side
 
     def w_wait(step):
-        src = (hp + 8 - step) % 8
+        src = shard_of(step)
         return pltpu.make_async_remote_copy(w_ref, wbuf.at[w_rows(2 * src + core)], w_s.at[step], w_r.at[src],
                                             device_id={"head": 2 * src + core}, device_id_type=MESH)
 
@@ -82,7 +110,7 @@
                                             device_id={"head": h + 1 - 2 * core}, device_id_type=MESH)
 
     def g_copy(step):
-        src = (hp + 8 - step) % 8
+        src = shard_of(step)
         rows = w_rows(2 * src + core)
         return pltpu.make_async_remote_copy(wbuf.at[rows], wbuf.at[rows], g_s.at[src], g_r.at[src],
                                             device_id={"head": h + 1 - 2 * core}, device_id_type=MESH)
@@ -100,24 +128,26 @@
         return pltpu.make_async_remote_copy(att.at[pl.ds(96 * j, 96)], abuf.at[j], a_s.at[j], a_r.at[j],
                                             device_id={"head": j}, device_id_type=MESH)
 
-    @pl.when(has_near)
-    def _():
-        q_copy(0).start()
-        q_copy(1).start()
+    for step in range(4):
+        w_copy(step).start()
+    g_own().start()
+
+    for g in range(4):
+        @pl.when(gets[g])
+        def _():
+            q_copy(g).start()
 
     @pl.when(gives_prev)
     def _():
         prev_copy(0).start()
         prev_copy(1).start()
 
-    @pl.when(d <= 7)
-    def _():
-        far_copy(0).start()
-        far_copy(1).start()
-
-    for step in range(1, 8):
-        w_copy(step).start()
-    g_own().start()
+    for w in range(2):
+        @pl.when(gives_far[w])
+        def _():
+            far_copy(w, 0).start()
+            far_copy(w, 1).start()
+
     wbuf[w_rows(h), :] = w_ref[...]
 
     lane = lax.broadcasted_iota(jnp.int32, (PR, 128), 1)
@@ -150,22 +180,21 @@
     for w in range(2):
         prep_q(w, q_ref[pl.ds(w * PR, PR), :])
         prep_kv(w, k_ref[pl.ds(w * PR, PR), :], v_ref[pl.ds(w * PR, PR), :], 2 * d + w)
-    for t in range(4):
+    for t in range(5):
         for par in range(2):
             acc[t, par, 0:80] = jnp.zeros((80, PR), F32)
             acc[t, par, 80:88] = jnp.full((8, PR), LOW, F32)
 
-    count = jnp.where(has_far, jnp.where(does_near, 8, 6), jnp.where(has_prev, 6, 5))
-
     def pair_of(i):
-        late = jnp.where(i == 3, 4, jnp.where(i == 4, 5, jnp.where(i == 5, 7, i)))
-        early = jnp.where(i == 4, jnp.where(has_prev, 4, 6), jnp.where(i == 5, 6, i))
-        return jnp.where(does_near, jnp.where(has_far, i, early), late)
+        return (order >> (4 * i)) & 15
+
+    query_of = sum(v << (3 * n) for n, v in enumerate((0, 1, 1, 2, 0, 0, 1, 3, 1, 4)))
+    key_of = sum(v << (3 * n) for n, v in enumerate((0, 1, 0, 0, 2, 3, 4, 1, 5, 0)))
 
     def slots(j):
-        q = jnp.where(j == 3, 2, jnp.where(j == 6, 3, jnp.where((j == 1) | (j == 2) | (j == 7), 1, 0)))
-        k = jnp.where(j == 4, 2, jnp.where(j == 5, 3, jnp.where(j == 7, 4, jnp.where((j == 1) | (j == 6), 1, 0))))
-        return q, k
+        q = (jnp.int32(query_of) >> (3 * j)) & 7
+        k = (jnp.int32(key_of) >> (3 * j)) & 7
+        return q, jnp.where((j == 9) & (d == 6), 1, k)
 
     chunks = [(c, p) for p in range(2) for c in range(NCH)]
 
@@ -196,17 +225,29 @@
         acc[q, par, 0:80] = acc[q, par, 0:80] * jnp.exp2(old - new) + total * jnp.exp2(m - new)
         acc[q, par, 80:88] = jnp.broadcast_to(new, (8, PR))
 
-    def put_near(w, par):
-        oout[w, 64 * par:64 * par + 64] = acc[2 + w, par, 0:64].astype(BF)
-
-    def put_stats(w):
+    def put_part(n, par):
+        oout[n, 64 * par:64 * par + 64] = acc[2 + n, par, 0:64].astype(BF)
+
+    def put_stats(n):
         parts = []
         for par in range(2):
-            l = acc[2 + w, par, 64:65]
+            l = acc[2 + n, par, 64:65]
             hi = l.astype(BF).astype(F32)
-            parts += [hi, l - hi, acc[2 + w, par, 80:81]]
+            parts += [hi, l - hi, acc[2 + n, par, 80:81]]
         pad = jnp.zeros((10, PR), F32)
-        oout[w, 128:144] = jnp.concatenate(parts + [pad], axis=0).astype(BF)
+        oout[n, 128:144] = jnp.concatenate(parts + [pad], axis=0).astype(BF)
+
+    def give_part(n, par):
+        put_part(n, par)
+        if par == 1:
+            put_stats(n)
+        for g in range(4):
+            if place[g] == n:
+                @pl.when(does[g])
+                def _():
+                    out_copy(g, par).start()
+
+    jobs = ((0, 3), (1, 7), (2, 9))
 
     top = None
     for c, p in chunks:
@@ -217,65 +258,88 @@
         j = pair_of(i)
         nxt = pair_of(jnp.minimum(i + 1, count - 1))
         fresh = i + 1 < count
-        for w, at in ((0, 3), (1, 6)):
+        for n in range(2):
+            @pl.when((i == n + 1) & has_prev)
+            def _():
+                prev_copy(n).wait_recv()
+
+                @pl.when(gives_relay)
+                def _():
+                    relay_copy(n).start()
+
+        for n, at in jobs:
             @pl.when(fresh & (nxt == at))
             def _():
-                q_copy(w).wait_recv()
-                prep_q(2 + w, qraw[pl.ds(w * PR, PR), :])
+                for g in range(4):
+                    if place[g] == n:
+                        @pl.when(does[g])
+                        def _():
+                            q_copy(g).wait_recv()
+                prep_q(2 + n, qraw[n])
 
         @pl.when(fresh & (nxt == 4))
         def _():
-            prev_copy(0).wait_recv()
-            prev_copy(1).wait_recv()
             prep_kv(2, kprev[...], vprev[...], 2 * d - 1)
 
-        @pl.when(fresh & (nxt == 5))
-        def _():
-            far_copy(0).wait_recv()
-            far_copy(1).wait_recv()
-            prep_kv(3, kfar[pl.ds(0, PR), :], vfar[pl.ds(0, PR), :], 2 * d - 16)
-            prep_kv(4, kfar[pl.ds(PR, PR), :], vfar[pl.ds(PR, PR), :], 2 * d - 15)
+        for w, at in ((0, 5), (1, 8)):
+            @pl.when(fresh & (nxt == at))
+            def _():
+                far_copy(w, 0).wait_recv()
+                far_copy(w, 1).wait_recv()
+                prep_kv((3, 5)[w], kfar[w], vfar[w], 2 * d - 16 + w)
+
+        @pl.when(fresh & (nxt == 6))
+        def _():
+            relay_copy(0).wait_recv()
+            relay_copy(1).wait_recv()
+            prep_kv(4, knear[...], vnear[...], 2 * d - 3)
 
         q, k = slots(j)
         qn, kn = slots(nxt)
         step(q, k, 0, s0, m0, q, k, 1, s1, m1)
-        for w, at in ((0, 3), (1, 6)):
+        for n, at in jobs:
             @pl.when(j == at)
             def _():
-                put_near(w, 0)
-                out_copy(w, 0).start()
+                give_part(n, 0)
         step(q, k, 1, s1, m1, qn, kn, 0, s0, m0)
-        for w, at in ((0, 3), (1, 6)):
+        for n, at in jobs:
             @pl.when(j == at)
             def _():
-                put_near(w, 1)
-                put_stats(w)
-                out_copy(w, 1).start()
+                give_part(n, 1)
+
+        @pl.when(i == 1)
+        def _():
+            w_wait(0).wait_recv()
+            for s in range(4, 7):
+                w_copy(s).start()
 
         @pl.when(i == 3)
         def _():
-            for s in range(1, 8):
-                w_wait(s).wait_recv()
+            for s in range(7):
+                if s:
+                    w_wait(s).wait_recv()
                 g_copy(s).start()
         return 0
 
     lax.fori_loop(0, count, body, 0)
 
-    for w in range(2):
-        @pl.when(has_near)
-        def _():
-            out_copy(w, 0).wait_recv()
-            out_copy(w, 1).wait_recv()
-            stats = oin[w, 128:144].astype(F32)
-            for par in range(2):
-                l = stats[3 * par:3 * par + 1] + stats[3 * par + 1:3 * par + 2]
-                m = stats[3 * par + 2:3 * par + 3]
-                part = oin[w, 64 * par:64 * par + 64].astype(F32)
-                old = acc[w, par, 80:81]
-                new = jnp.maximum(old, m)
-                fo, fn = jnp.exp2(old - new), jnp.exp2(m - new)
-                acc[w, par, 0:64] = acc[w, par, 0:64] * fo + part * fn
-                acc[w, par, 64:65] = acc[w, par, 64:65] * fo + l * fn
+    for w in (1, 0):
+        for g in ((0, 2), (1, 3))[w]:
+            @pl.when(gets[g])
+            def _():
+                out_copy(g, 0).wait_recv()
+                out_copy(g, 1).wait_recv()
+                stats = oin[g, 128:144].astype(F32)
+                for par in range(2):
+                    l = stats[3 * par:3 * par + 1] + stats[3 * par + 1:3 * par + 2]
+                    m = stats[3 * par + 2:3 * par + 3]
+                    part = oin[g, 64 * par:64 * par + 64].astype(F32)
+                    old = acc[w, par, 80:81]
+                    new = jnp.maximum(old, m)
+                    fo, fn = jnp.exp2(old - new), jnp.exp2(m - new)
+                    acc[w, par, 0:64] = acc[w, par, 0:64] * fo + part * fn
+                    acc[w, par, 64:65] = acc[w, par, 64:65] * fo + l * fn
+                    acc[w, par, 80:81] = new
         halves = []
         for par in range(2):
             halves.append((acc[w, par, 0:64] * (1.0 / acc[w, par, 64:65])).astype(BF))
@@ -305,29 +369,34 @@
     o_ref[:, 0:1024] = out[0:96]
     o_ref[:, 1024:2048] = out[96:192]
 
-    @pl.when(has_near)
-    def _():
-        q_copy(0).wait_send()
-        q_copy(1).wait_send()
+    for g in range(4):
+        @pl.when(gets[g])
+        def _():
+            q_copy(g).wait_send()
+
+        @pl.when(does[g])
+        def _():
+            out_copy(g, 0).wait_send()
+            out_copy(g, 1).wait_send()
 
     @pl.when(gives_prev)
     def _():
         prev_copy(0).wait_send()
         prev_copy(1).wait_send()
 
-    @pl.when(d <= 7)
+    @pl.when(gives_relay)
     def _():
-        far_copy(0).wait_send()
-        far_copy(1).wait_send()
-
-    @pl.when(does_near)
-    def _():
-        for w in range(2):
-            for par in range(2):
-                out_copy(w, par).wait_send()
+        relay_copy(0).wait_send()
+        relay_copy(1).wait_send()
+
+    for w in range(2):
+        @pl.when(gives_far[w])
+        def _():
+            far_copy(w, 0).wait_send()
+            far_copy(w, 1).wait_send()
 
     g_own().wait_send()
-    for s in range(1, 8):
+    for s in range(7):
         w_copy(s).wait_send()
         g_copy(s).wait_send()
     for j in range(16):
@@ -346,27 +415,29 @@
         in_specs=[vmem, vmem, vmem, smem, vmem],
         out_specs=vmem,
         scratch_shapes=[
-            pltpu.VMEM((2 * PR, 128), BF),
+            pltpu.VMEM((3, PR, 128), BF),
             pltpu.VMEM((PR, 128), BF),
             pltpu.VMEM((PR, 128), BF),
-            pltpu.VMEM((2 * PR, 128), BF),
-            pltpu.VMEM((2 * PR, 128), BF),
-            pltpu.VMEM((4, 2, 2, 256, PR), BF),
-            pltpu.VMEM((5, PR, 128), BF),
-            pltpu.VMEM((5, 2, 80, PR), BF),
+            pltpu.VMEM((PR, 128), BF),
+            pltpu.VMEM((PR, 128), BF),
+            pltpu.VMEM((2, PR, 128), BF),
+            pltpu.VMEM((2, PR, 128), BF),
+            pltpu.VMEM((5, 2, 2, 256, PR), BF),
+            pltpu.VMEM((6, PR, 128), BF),
+            pltpu.VMEM((6, 2, 80, PR), BF),
             pltpu.VMEM((2 * PR, PR), F32),
             pltpu.VMEM((2 * PR, PR), F32),
             pltpu.VMEM((8, PR), F32),
             pltpu.VMEM((8, PR), F32),
-            pltpu.VMEM((4, 2, 88, PR), F32),
-            pltpu.VMEM((2, 144, PR), BF),
-            pltpu.VMEM((2, 144, PR), BF),
+            pltpu.VMEM((5, 2, 88, PR), F32),
+            pltpu.VMEM((3, 144, PR), BF),
+            pltpu.VMEM((4, 144, PR), BF),
             pltpu.VMEM((1024, 1024), BF),
             pltpu.VMEM((2 * PR, 128), BF),
             pltpu.VMEM((16, 96, 128), BF),
             pltpu.VMEM((192, 1024), BF),
-            dma((2,)), dma((2,)), dma((2,)), dma((2,)), dma((2,)), dma((2,)),
-            dma((4,)), dma((4,)), dma((8,)), dma((8,)), dma((8,)), dma((8,)),
+            dma((4,)), dma((4,)), dma((2,)), dma((2,)), dma((2,)), dma((2,)), dma((4,)), dma((4,)),
+            dma((8,)), dma((8,)), dma((8,)), dma((8,)), dma((8,)), dma((8,)),
             dma((16,)), dma((16,)),
         ],
         compiler_params=pltpu.CompilerParams(collective_id=0, has_side_effects=True),

time: 67.8 us -> 59 us (0.87)
  the two profiles are of different devices: /device:TPU:89 before, /device:TPU:5 now
where the time goes in v2:
time: 59 us; the launch traced here: 58.7 us
  Pallas kernels  56.8 us (96%)
  local copies, waits for them, and re-layouts  1.87 us (3%)
    pallas_call x1, Pallas kernels, shards(): pl.pallas_call(kernel, out_shape=jax.ShapeDtypeStruct((96, 2048), BF), in...  56.8 us
    reshape x1, local copies, waits for them, and re-layouts, shards(): return out.reshape(192, 1024)  1.87 us

profile of v2, /device:TPU:5, one launch (start us, length us, event | category | flops | bytes accessed | tf_op | source)
XLA Modules:
  0.0 58.7 jit_solution(1006952896094954165)
XLA Ops:
  0.0 56.8 %fused.1 = bf16[96,2048]{1,0:T(8,128)(2,1)} custom-call(bf16[1536,128]{1,0:T(8,128)(2,1)} %bitcast.3, bf16[1536,128]{1,0:T(8,128)(2,1)} %bitcast.4, bf16[1536,128]{1,0:T(8,128)(2,1)} %bitcast.5, s32[32]{0:T(128)} %len_ref.1, bf16[64,1024]{1,0:T(8,128)(2,1)} %w_ref.1), custom_call_target="tpu_custom_call" | custom-call | tf_op jit(solution)/shard_map/fused/pallas_call | solution.py:412
  56.9 1.9 %reshape.3 = bf16[192,1024]{1,0:T(8,128)(2,1)} reshape(bf16[96,2048]{1,0:T(8,128)(2,1)} %fused.1) | data formatting | bytes 786432 | tf_op jit(solution)/shard_map/reshape | solution.py:446

commit v3 on v2

--- a/solution.py
+++ b/solution.py
@@ -17,35 +17,31 @@
 
 
 def kernel(q_ref, k_ref, v_ref, len_ref, w_ref, o_ref,
-           qraw, kprev, vprev, knear, vnear, kfar, vfar, qt, ka, vt, s0, s1, m0, m1, acc,
+           qraw, kprev, vprev, knear, vnear, kpass, vpass, kfar, vfar, qt, ka, vt, s0, s1, m0, m1, acc,
            oout, oin, wbuf, att, abuf, xbuf,
-           q_s, q_r, p_s, p_r, n_s, n_r, f_s, f_r, o_s, o_r, w_s, w_r, g_s, g_r, a_s, a_r):
+           q_s, q_r, p_s, p_r, n_s, n_r, z_s, z_r, f_s, f_r, o_s, o_r, w_s, w_r, g_s, g_r, a_s, a_r):
     d = lax.axis_index("frame")
     h = lax.axis_index("head")
     hp = h // 2
     core = h % 2
     side = hp % 2
     line = hp // 2
-    does = (d <= 13, (d <= 7) & (d != 6), d == 0, d == 6)
-    gets = (d >= 2, (d >= 8) & (d != 14), d == 8, d == 8)
-    away = (2, 8, 8, 2)
-    place = (0, 1, 2, 2)
+    does = (d <= 13, d <= 7)
+    gets = (d >= 2, d >= 8)
+    away = (2, 8)
+    half = (0, 1)
     has_prev = d >= 1
     gives_prev = d <= 14
-    has_relay = (d >= 2) & (d != 8)
     gives_relay = (d >= 1) & (d <= 14) & (d != 7)
-    has_far = (d >= 9, d == 14)
-    gives_far = ((d >= 1) & (d <= 7), d == 6)
+    gives_far = d <= 7
 
     def digits(values):
         return sum(v << (4 * n) for n, v in enumerate(values))
 
     order = jnp.where(d <= 7, digits((0, 1, 2, 3, 4, 7, 6)), digits((0, 1, 2, 3, 4, 5, 6)))
-    order = jnp.where(d == 0, digits((0, 1, 2, 3, 7, 9)), order)
-    order = jnp.where(d == 6, digits((0, 1, 2, 3, 9, 4, 6)), order)
-    order = jnp.where(d == 14, digits((0, 1, 2, 4, 5, 8, 6)), order)
-    order = jnp.where(d == 15, digits((0, 1, 2, 4, 5, 6)), order)
-    count = jnp.where((d <= 1) | (d == 15), 6, jnp.where(d == 8, 5, 7))
+    order = jnp.where(d == 0, digits((0, 1, 2, 3, 7)), order)
+    order = jnp.where(d >= 14, digits((0, 1, 2, 4, 5, 6)), order)
+    count = jnp.where(d == 0, 5, jnp.where((d == 1) | (d >= 14), 6, 7))
 
     bar = pltpu.get_barrier_semaphore()
     for shift in (1, 2, 8):
@@ -58,11 +54,12 @@
             pl.semaphore_signal(bar, inc=1, device_id={"frame": d + shift}, device_id_type=MESH)
     for step in range(1, 16):
         pl.semaphore_signal(bar, inc=1, device_id={"head": (h + step) % 16}, device_id_type=MESH)
-    one = lambda c: jnp.where(c, 1, 0)
-    pl.semaphore_wait(bar, 16 + one(d >= 1) + one(d <= 14) + one(d >= 2) + one(d <= 13))
+    @pl.when((d == 8) | (d == 15))
+    def _():
+        pl.semaphore_signal(bar, inc=1, device_id={"frame": jnp.where(d == 8, 15, 8)}, device_id_type=MESH)
 
     def q_copy(g):
-        return pltpu.make_async_remote_copy(q_ref.at[pl.ds((0, 1, 0, 1)[g] * PR, PR)], qraw.at[place[g]], q_s.at[g], q_r.at[g],
+        return pltpu.make_async_remote_copy(q_ref.at[pl.ds(half[g] * PR, PR)], qraw.at[g], q_s.at[g], q_r.at[g],
                                             device_id={"frame": d - away[g]}, device_id_type=MESH)
 
     def prev_copy(n):
@@ -75,14 +72,24 @@
         return pltpu.make_async_remote_copy(src, dst, n_s.at[n], n_r.at[n],
                                             device_id={"frame": d + 1}, device_id_type=MESH)
 
-    def far_copy(w, n):
+    def pass_copy(n):
+        src, dst = ((kprev, kpass), (vprev, vpass))[n]
+        return pltpu.make_async_remote_copy(src, dst, z_s.at[n], z_r.at[n],
+                                            device_id={"frame": d + 8}, device_id_type=MESH)
+
+    def hand_copy(n):
+        src, dst = ((kpass, knear), (vpass, vnear))[n]
+        return pltpu.make_async_remote_copy(src, dst, n_s.at[n], n_r.at[n],
+                                            device_id={"frame": d - 7}, device_id_type=MESH)
+
+    def far_copy(n):
         src, dst = ((k_ref, kfar), (v_ref, vfar))[n]
-        return pltpu.make_async_remote_copy(src.at[pl.ds(w * PR, PR)], dst.at[w], f_s.at[2 * w + n], f_r.at[2 * w + n],
+        return pltpu.make_async_remote_copy(src.at[pl.ds(0, PR)], dst, f_s.at[n], f_r.at[n],
                                             device_id={"frame": d + 8}, device_id_type=MESH)
 
     def out_copy(g, par):
         lo, n = ((0, 64), (64, 80))[par]
-        return pltpu.make_async_remote_copy(oout.at[place[g], pl.ds(lo, n)], oin.at[g, pl.ds(lo, n)],
+        return pltpu.make_async_remote_copy(oout.at[g, pl.ds(lo, n)], oin.at[g, pl.ds(lo, n)],
                                             o_s.at[2 * g + par], o_r.at[2 * g + par],
                                             device_id={"frame": d + away[g]}, device_id_type=MESH)
 
@@ -120,33 +127,18 @@
         return pltpu.make_async_remote_copy(wbuf.at[rows], wbuf.at[rows], g_s.at[src], g_r.at[src],
                                             device_id={"head": h + 1 - 2 * core}, device_id_type=MESH)
 
-    def a_copy(j):
-        return pltpu.make_async_remote_copy(att.at[pl.ds(96 * j, 96)], abuf.at[h], a_s.at[j], a_r.at[h],
+    def peer(w, k):
+        return 8 * w + (h + k) % 8
+
+    def a_copy(w, k):
+        j = peer(w, k)
+        return pltpu.make_async_remote_copy(att.at[pl.ds(pl.multiple_of(96 * j, 32), 96)], abuf.at[h],
+                                            a_s.at[8 * w + k], a_r.at[h],
                                             device_id={"head": j}, device_id_type=MESH)
 
     def a_wait(j):
         return pltpu.make_async_remote_copy(att.at[pl.ds(96 * j, 96)], abuf.at[j], a_s.at[j], a_r.at[j],
                                             device_id={"head": j}, device_id_type=MESH)
-
-    for step in range(4):
-        w_copy(step).start()
-    g_own().start()
-
-    for g in range(4):
-        @pl.when(gets[g])
-        def _():
-            q_copy(g).start()
-
-    @pl.when(gives_prev)
-    def _():
-        prev_copy(0).start()
-        prev_copy(1).start()
-
-    for w in range(2):
-        @pl.when(gives_far[w])
-        def _():
-            far_copy(w, 0).start()
-            far_copy(w, 1).start()
 
     wbuf[w_rows(h), :] = w_ref[...]
 
@@ -169,32 +161,55 @@
         x = queries.astype(F32) * SCALE
         hi = x.astype(BF)
         low = (x - hi.astype(F32))
-        for n, part in enumerate((hi.astype(F32), low)):
-            swapped = pltpu.roll(part, 64, 1)
-            rows = slice(128 * n, 128 * n + 128)
-            qt[slot, 0, 0, rows] = jnp.where(lane < 64, part, 0.0).astype(BF).T
-            qt[slot, 0, 1, rows] = jnp.where(lane < 64, 0.0, swapped).astype(BF).T
-            qt[slot, 1, 0, rows] = jnp.where(lane < 64, swapped, 0.0).astype(BF).T
-            qt[slot, 1, 1, rows] = jnp.where(lane < 64, 0.0, part).astype(BF).T
+        for n, part in enumerate((hi, low.astype(BF))):
+            turned = part.T
+            for par in range(2):
+                rows = turned[64 * par:64 * par + 64]
+                for p in range(2):
+                    at = 128 * n + 64 * p
+                    qt[slot, par, p, at:at + 64] = rows
+                    at = 128 * n + 64 - 64 * p
+                    qt[slot, par, p, at:at + 64] = jnp.zeros((64, PR), BF)
 
     for w in range(2):
         prep_q(w, q_ref[pl.ds(w * PR, PR), :])
         prep_kv(w, k_ref[pl.ds(w * PR, PR), :], v_ref[pl.ds(w * PR, PR), :], 2 * d + w)
-    for t in range(5):
+    for t in range(4):
         for par in range(2):
             acc[t, par, 0:80] = jnp.zeros((80, PR), F32)
             acc[t, par, 80:88] = jnp.full((8, PR), LOW, F32)
 
+    one = lambda c: jnp.where(c, 1, 0)
+    pl.semaphore_wait(bar, 16 + one(d >= 1) + one(d <= 14) + one(d >= 2) + one(d <= 13) + one((d == 8) | (d == 15)))
+    for step in range(4):
+        w_copy(step).start()
+    g_own().start()
+
+    for g in range(2):
+        @pl.when(gets[g])
+        def _():
+            q_copy(g).start()
+
+    @pl.when(gives_prev)
+    def _():
+        prev_copy(0).start()
+        prev_copy(1).start()
+
+    @pl.when(gives_far)
+    def _():
+        far_copy(0).start()
+        far_copy(1).start()
+
     def pair_of(i):
         return (order >> (4 * i)) & 15
 
-    query_of = sum(v << (3 * n) for n, v in enumerate((0, 1, 1, 2, 0, 0, 1, 3, 1, 4)))
-    key_of = sum(v << (3 * n) for n, v in enumerate((0, 1, 0, 0, 2, 3, 4, 1, 5, 0)))
+    query_of = sum(v << (3 * n) for n, v in enumerate((0, 1, 1, 2, 0, 0, 1, 3)))
+    key_of = sum(v << (3 * n) for n, v in enumerate((0, 1, 0, 0, 2, 3, 4, 1)))
 
     def slots(j):
         q = (jnp.int32(query_of) >> (3 * j)) & 7
         k = (jnp.int32(key_of) >> (3 * j)) & 7
-        return q, jnp.where((j == 9) & (d == 6), 1, k)
+        return q, k
 
     chunks = [(c, p) for p in range(2) for c in range(NCH)]
 
@@ -241,13 +256,9 @@
         put_part(n, par)
         if par == 1:
             put_stats(n)
-        for g in range(4):
-            if place[g] == n:
-                @pl.when(does[g])
-                def _():
-                    out_copy(g, par).start()
-
-    jobs = ((0, 3), (1, 7), (2, 9))
+        out_copy(n, par).start()
+
+    jobs = ((0, 3), (1, 7))
 
     top = None
     for c, p in chunks:
@@ -267,26 +278,30 @@
                 def _():
                     relay_copy(n).start()
 
+                @pl.when(d == 7)
+                def _():
+                    pass_copy(n).start()
+
+            @pl.when((i == n + 3) & (d == 15))
+            def _():
+                pass_copy(n).wait_recv()
+                hand_copy(n).start()
+
         for n, at in jobs:
             @pl.when(fresh & (nxt == at))
             def _():
-                for g in range(4):
-                    if place[g] == n:
-                        @pl.when(does[g])
-                        def _():
-                            q_copy(g).wait_recv()
+                q_copy(n).wait_recv()
                 prep_q(2 + n, qraw[n])
 
         @pl.when(fresh & (nxt == 4))
         def _():
             prep_kv(2, kprev[...], vprev[...], 2 * d - 1)
 
-        for w, at in ((0, 5), (1, 8)):
-            @pl.when(fresh & (nxt == at))
-            def _():
-                far_copy(w, 0).wait_recv()
-                far_copy(w, 1).wait_recv()
-                prep_kv((3, 5)[w], kfar[w], vfar[w], 2 * d - 16 + w)
+        @pl.when(fresh & (nxt == 5))
+        def _():
+            far_copy(0).wait_recv()
+            far_copy(1).wait_recv()
+            prep_kv(3, kfar[...], vfar[...], 2 * d - 16)
 
         @pl.when(fresh & (nxt == 6))
         def _():
@@ -324,7 +339,7 @@
     lax.fori_loop(0, count, body, 0)
 
     for w in (1, 0):
-        for g in ((0, 2), (1, 3))[w]:
+        for g in (w,):
             @pl.when(gets[g])
             def _():
                 out_copy(g, 0).wait_recv()
@@ -344,32 +359,38 @@
         for par in range(2):
             halves.append((acc[w, par, 0:64] * (1.0 / acc[w, par, 64:65])).astype(BF))
         att[pl.ds(w * PR, PR), :] = jnp.concatenate(halves, axis=0).T
-        for j in range(8 * w, 8 * w + 8):
-            @pl.when(h == j)
-            def _():
-                abuf[j] = att[96 * j:96 * j + 96, :]
-
-            @pl.when(h != j)
-            def _():
-                a_copy(j).start()
+        for k in range(1, 8):
+            a_copy(w, k).start()
+
+        @pl.when(h // 8 == w)
+        def _():
+            abuf[h] = att[pl.ds(pl.multiple_of(96 * h, 32), 96), :]
+
+        @pl.when(h // 8 != w)
+        def _():
+            a_copy(w, 0).start()
 
     for src in range(8):
         g_wait(src).wait_recv()
     low_half = lax.broadcasted_iota(jnp.int32, (96, 128), 1) < 64
-    for n in range(8):
-        for j in (2 * n, 2 * n + 1):
-            @pl.when(h != j)
-            def _():
-                a_wait(j).wait_recv()
-        a = abuf[2 * n].astype(F32)
-        b = abuf[2 * n + 1].astype(F32)
-        xbuf[0:96, 128 * n:128 * n + 128] = jnp.where(low_half, a, pltpu.roll(b, 64, 1)).astype(BF)
-        xbuf[96:192, 128 * n:128 * n + 128] = jnp.where(low_half, pltpu.roll(a, 64, 1), b).astype(BF)
-    out = jnp.dot(xbuf[...], wbuf[...], preferred_element_type=F32).astype(BF)
+    total = None
+    for part in range(4):
+        for n in (2 * part, 2 * part + 1):
+            for j in (2 * n, 2 * n + 1):
+                @pl.when(h != j)
+                def _():
+                    a_wait(j).wait_recv()
+            a = abuf[2 * n].astype(F32)
+            b = abuf[2 * n + 1].astype(F32)
+            xbuf[0:96, 128 * n:128 * n + 128] = jnp.where(low_half, a, pltpu.roll(b, 64, 1)).astype(BF)
+            xbuf[96:192, 128 * n:128 * n + 128] = jnp.where(low_half, pltpu.roll(a, 64, 1), b).astype(BF)
+        some = jnp.dot(xbuf[:, 256 * part:256 * part + 256], wbuf[256 * part:256 * part + 256], preferred_element_type=F32)
+        total = some if total is None else total + some
+    out = total.astype(BF)
     o_ref[:, 0:1024] = out[0:96]
     o_ref[:, 1024:2048] = out[96:192]
 
-    for g in range(4):
+    for g in range(2):
         @pl.when(gets[g])
         def _():
             q_copy(g).wait_send()
@@ -389,20 +410,32 @@
         relay_copy(0).wait_send()
         relay_copy(1).wait_send()
 
-    for w in range(2):
-        @pl.when(gives_far[w])
-        def _():
-            far_copy(w, 0).wait_send()
-            far_copy(w, 1).wait_send()
+    @pl.when(d == 7)
+    def _():
+        pass_copy(0).wait_send()
+        pass_copy(1).wait_send()
+
+    @pl.when(d == 15)
+    def _():
+        hand_copy(0).wait_send()
+        hand_copy(1).wait_send()
+
+    @pl.when(gives_far)
+    def _():
+        far_copy(0).wait_send()
+        far_copy(1).wait_send()
 
     g_own().wait_send()
     for s in range(7):
         w_copy(s).wait_send()
         g_copy(s).wait_send()
-    for j in range(16):
-        @pl.when(h != j)
-        def _():
-            a_copy(j).wait_send()
+    for w in range(2):
+        for k in range(1, 8):
+            a_copy(w, k).wait_send()
+
+        @pl.when(h // 8 != w)
+        def _():
+            a_copy(w, 0).wait_send()
 
 
 def shards(query_proj, key_proj, value_proj, lengths, out_weight):
@@ -415,29 +448,31 @@
         in_specs=[vmem, vmem, vmem, smem, vmem],
         out_specs=vmem,
         scratch_shapes=[
-            pltpu.VMEM((3, PR, 128), BF),
-            pltpu.VMEM((PR, 128), BF),
-            pltpu.VMEM((PR, 128), BF),
-            pltpu.VMEM((PR, 128), BF),
-            pltpu.VMEM((PR, 128), BF),
             pltpu.VMEM((2, PR, 128), BF),
-            pltpu.VMEM((2, PR, 128), BF),
-            pltpu.VMEM((5, 2, 2, 256, PR), BF),
-            pltpu.VMEM((6, PR, 128), BF),
-            pltpu.VMEM((6, 2, 80, PR), BF),
+            pltpu.VMEM((PR, 128), BF),
+            pltpu.VMEM((PR, 128), BF),
+            pltpu.VMEM((PR, 128), BF),
+            pltpu.VMEM((PR, 128), BF),
+            pltpu.VMEM((PR, 128), BF),
+            pltpu.VMEM((PR, 128), BF),
+            pltpu.VMEM((PR, 128), BF),
+            pltpu.VMEM((PR, 128), BF),
+            pltpu.VMEM((4, 2, 2, 256, PR), BF),
+            pltpu.VMEM((5, PR, 128), BF),
+            pltpu.VMEM((5, 2, 80, PR), BF),
             pltpu.VMEM((2 * PR, PR), F32),
             pltpu.VMEM((2 * PR, PR), F32),
             pltpu.VMEM((8, PR), F32),
             pltpu.VMEM((8, PR), F32),
-            pltpu.VMEM((5, 2, 88, PR), F32),
-            pltpu.VMEM((3, 144, PR), BF),
-            pltpu.VMEM((4, 144, PR), BF),
+            pltpu.VMEM((4, 2, 88, PR), F32),
+            pltpu.VMEM((2, 144, PR), BF),
+            pltpu.VMEM((2, 144, PR), BF),
             pltpu.VMEM((1024, 1024), BF),
             pltpu.VMEM((2 * PR, 128), BF),
             pltpu.VMEM((16, 96, 128), BF),
             pltpu.VMEM((192, 1024), BF),
-            dma((4,)), dma((4,)), dma((2,)), dma((2,)), dma((2,)), dma((2,)), dma((4,)), dma((4,)),
-            dma((8,)), dma((8,)), dma((8,)), dma((8,)), dma((8,)), dma((8,)),
+            dma((2,)), dma((2,)), dma((2,)), dma((2,)), dma((2,)), dma((2,)), dma((2,)), dma((2,)), dma((2,)), dma((2,)),
+            dma((4,)), dma((4,)), dma((8,)), dma((8,)), dma((8,)), dma((8,)),
             dma((16,)), dma((16,)),
         ],
         compiler_params=pltpu.CompilerParams(collective_id=0, has_side_effects=True),

time: 59 us -> 53 us (0.90)
  Pallas kernels: 56.8 us -> 51 us
    pallas_call x1, Pallas kernels: 56.8 us -> 51 us  [shards(): pl.pallas_call(kernel, out_shape=jax.ShapeDtypeStruct((96, 2048), BF), in...]
where the time goes in v3:
time: 53 us; the launch traced here: 52.8 us
  Pallas kernels  51 us (96%)
  local copies, waits for them, and re-layouts  1.87 us (4%)
    pallas_call x1, Pallas kernels, shards(): pl.pallas_call(kernel, out_shape=jax.ShapeDtypeStruct((96, 2048), BF), in...  51 us
    reshape x1, local copies, waits for them, and re-layouts, shards(): return out.reshape(192, 1024)  1.87 us

profile of v3, /device:TPU:5, one launch (start us, length us, event | category | flops | bytes accessed | tf_op | source)
XLA Modules:
  0.0 52.8 jit_solution(8249989315326721096)
XLA Ops:
  0.0 51.0 %fused.1 = bf16[96,2048]{1,0:T(8,128)(2,1)} custom-call(bf16[1536,128]{1,0:T(8,128)(2,1)} %bitcast.3, bf16[1536,128]{1,0:T(8,128)(2,1)} %bitcast.4, bf16[1536,128]{1,0:T(8,128)(2,1)} %bitcast.5, s32[32]{0:T(128)} %len_ref.1, bf16[64,1024]{1,0:T(8,128)(2,1)} %w_ref.1), custom_call_target="tpu_custom_call" | custom-call | tf_op jit(solution)/shard_map/fused/pallas_call | solution.py:445
  51.0 1.9 %reshape.3 = bf16[192,1024]{1,0:T(8,128)(2,1)} reshape(bf16[96,2048]{1,0:T(8,128)(2,1)} %fused.1) | data formatting | bytes 786432 | tf_op jit(solution)/shard_map/reshape | solution.py:481

commit v4 on v3

--- a/solution.py
+++ b/solution.py
@@ -287,28 +287,6 @@
                 pass_copy(n).wait_recv()
                 hand_copy(n).start()
 
-        for n, at in jobs:
-            @pl.when(fresh & (nxt == at))
-            def _():
-                q_copy(n).wait_recv()
-                prep_q(2 + n, qraw[n])
-
-        @pl.when(fresh & (nxt == 4))
-        def _():
-            prep_kv(2, kprev[...], vprev[...], 2 * d - 1)
-
-        @pl.when(fresh & (nxt == 5))
-        def _():
-            far_copy(0).wait_recv()
-            far_copy(1).wait_recv()
-            prep_kv(3, kfar[...], vfar[...], 2 * d - 16)
-
-        @pl.when(fresh & (nxt == 6))
-        def _():
-            relay_copy(0).wait_recv()
-            relay_copy(1).wait_recv()
-            prep_kv(4, knear[...], vnear[...], 2 * d - 3)
-
         q, k = slots(j)
         qn, kn = slots(nxt)
         step(q, k, 0, s0, m0, q, k, 1, s1, m1)
@@ -316,6 +294,28 @@
             @pl.when(j == at)
             def _():
                 give_part(n, 0)
+        for n, at in jobs:
+            @pl.when(fresh & (nxt == at))
+            def _():
+                q_copy(n).wait_recv()
+                prep_q(2 + n, qraw[n])
+
+        @pl.when(fresh & (nxt == 4))
+        def _():
+            prep_kv(2, kprev[...], vprev[...], 2 * d - 1)
+
+        @pl.when(fresh & (nxt == 5))
+        def _():
+            far_copy(0).wait_recv()
+            far_copy(1).wait_recv()
+            prep_kv(3, kfar[...], vfar[...], 2 * d - 16)
+
+        @pl.when(fresh & (nxt == 6))
+        def _():
+            relay_copy(0).wait_recv()
+            relay_copy(1).wait_recv()
+            prep_kv(4, knear[...], vnear[...], 2 * d - 3)
+
         step(q, k, 1, s1, m1, qn, kn, 0, s0, m0)
         for n, at in jobs:
             @pl.when(j == at)

time: 53 us -> 51.7 us (0.975)
  Pallas kernels: 51 us -> 49.7 us
    pallas_call x1, Pallas kernels: 51 us -> 49.7 us  [shards(): pl.pallas_call(kernel, out_shape=jax.ShapeDtypeStruct((96, 2048), BF), in...]
where the time goes in v4:
time: 51.7 us; the launch traced here: 51.6 us
  Pallas kernels  49.7 us (96%)
  local copies, waits for them, and re-layouts  1.87 us (4%)
    pallas_call x1, Pallas kernels, shards(): pl.pallas_call(kernel, out_shape=jax.ShapeDtypeStruct((96, 2048), BF), in...  49.7 us
    reshape x1, local copies, waits for them, and re-layouts, shards(): return out.reshape(192, 1024)  1.87 us

profile of v4, /device:TPU:5, one launch (start us, length us, event | category | flops | bytes accessed | tf_op | source)
XLA Modules:
  0.0 51.6 jit_solution(16486794614901720846)
XLA Ops:
  0.0 49.7 %fused.1 = bf16[96,2048]{1,0:T(8,128)(2,1)} custom-call(bf16[1536,128]{1,0:T(8,128)(2,1)} %bitcast.3, bf16[1536,128]{1,0:T(8,128)(2,1)} %bitcast.4, bf16[1536,128]{1,0:T(8,128)(2,1)} %bitcast.5, s32[32]{0:T(128)} %len_ref.1, bf16[64,1024]{1,0:T(8,128)(2,1)} %w_ref.1), custom_call_target="tpu_custom_call" | custom-call | tf_op jit(solution)/shard_map/fused/pallas_call | solution.py:445
  49.7 1.9 %reshape.3 = bf16[192,1024]{1,0:T(8,128)(2,1)} reshape(bf16[96,2048]{1,0:T(8,128)(2,1)} %fused.1) | data formatting | bytes 786432 | tf_op jit(solution)/shard_map/reshape | solution.py:481

commit v5 on v4

--- a/solution.py
+++ b/solution.py
@@ -38,7 +38,7 @@
     def digits(values):
         return sum(v << (4 * n) for n, v in enumerate(values))
 
-    order = jnp.where(d <= 7, digits((0, 1, 2, 3, 4, 7, 6)), digits((0, 1, 2, 3, 4, 5, 6)))
+    order = jnp.where(d <= 7, digits((0, 1, 2, 3, 7, 4, 6)), digits((0, 1, 2, 3, 4, 5, 6)))
     order = jnp.where(d == 0, digits((0, 1, 2, 3, 7)), order)
     order = jnp.where(d >= 14, digits((0, 1, 2, 4, 5, 6)), order)
     count = jnp.where(d == 0, 5, jnp.where((d == 1) | (d >= 14), 6, 7))

time: 51.7 us -> 51.4 us (level)
  no operation moved by 1% of the time
where the time goes in v5:
time: 51.4 us; the launch traced here: 51.2 us
  Pallas kernels  49.3 us (96%)
  local copies, waits for them, and re-layouts  1.87 us (4%)
    pallas_call x1, Pallas kernels, shards(): pl.pallas_call(kernel, out_shape=jax.ShapeDtypeStruct((96, 2048), BF), in...  49.3 us
    reshape x1, local copies, waits for them, and re-layouts, shards(): return out.reshape(192, 1024)  1.87 us

profile of v5, /device:TPU:5, one launch (start us, length us, event | category | flops | bytes accessed | tf_op | source)
XLA Modules:
  0.0 51.2 jit_solution(10982940274623030187)
XLA Ops:
  0.0 49.3 %fused.1 = bf16[96,2048]{1,0:T(8,128)(2,1)} custom-call(bf16[1536,128]{1,0:T(8,128)(2,1)} %bitcast.3, bf16[1536,128]{1,0:T(8,128)(2,1)} %bitcast.4, bf16[1536,128]{1,0:T(8,128)(2,1)} %bitcast.5, s32[32]{0:T(128)} %len_ref.1, bf16[64,1024]{1,0:T(8,128)(2,1)} %w_ref.1), custom_call_target="tpu_custom_call" | custom-call | tf_op jit(solution)/shard_map/fused/pallas_call | solution.py:445
  49.4 1.9 %reshape.3 = bf16[192,1024]{1,0:T(8,128)(2,1)} reshape(bf16[96,2048]{1,0:T(8,128)(2,1)} %fused.1) | data formatting | bytes 786432 | tf_op jit(solution)/shard_map/reshape | solution.py:481
